TPU v7x, 32 devices: a whole 2x2x4 slice. The times are simulated.
32 devices in a mesh: dp: 4 (over z), seq: 8 (over y, x, core).
Axes of the slice: x: 2, y: 2, z: 4, core: 2. Of those that a mesh axis runs over, the one named last changes fastest.
Arguments:
- patches: bfloat16 [6144, 1280], P(('dp', 'seq')), may hold values from -6 to 6
- query_key_value: bfloat16 [6144, 3840], P(('dp', 'seq')), may hold values from -100 to 100
- counts: int32 [32, 4], P(('dp', 'seq')), may hold values from 4 to 48, as said below
- owner_index: int32 [1536, 1], P(('dp', 'seq')), may hold values from 0 to 7; in each aligned block of 48 rows (0 to 47, 48 to 95, ...) at most 6 rows name the same one
- out_weight: bfloat16 [1280, 1280], P(None, 'dp'), may hold values from -0.15625 to 0.15625
- ln_gain: float32 [1280], replicated, may hold values from 0.25 to 1.75
- ln_bias: float32 [1280], replicated, may hold values from -3 to 3
Outputs:
- image_tokens: bfloat16 [1536, 5120], P(('dp', 'seq'))
Inputs may be any that keep to these rules, and one draw needn't show every extreme that they name: Every count is a multiple of 4, each device's counts sum to at most 192, and some device's counts sum to exactly 192. `owner_index`: among the merge groups of one device, at most 6 name the same owner.
All inputs are finite; a program needn't handle non-finite values.
Results may differ from a plain program's by a relative error of at most 0.0029.
Values may be sent and summed in bfloat16 or wider, within the bound.
A program may use at most 64 MiB of HBM per device.

v0:
```python
import jax
import jax.numpy as jnp
from jax import lax
from jax.sharding import PartitionSpec as P

HEADS = 16
IMGS = 4


def segment_rows(count_row, row_count):
    image_ends = jnp.cumsum(count_row)
    row_ids = jnp.arange(row_count, dtype=jnp.int32)
    return jnp.sum((row_ids[:, None] >= image_ends[None, :]).astype(jnp.int32), axis=1)


def attend(packed, segment_ids, model_width):
    row_count = packed.shape[0]
    head_size = model_width // HEADS
    queries = packed[:, :model_width].reshape(row_count, HEADS, head_size)
    keys_all = packed[:, model_width : 2 * model_width].reshape(row_count, HEADS, head_size)
    values_all = packed[:, 2 * model_width :].reshape(row_count, HEADS, head_size)
    scores = jnp.einsum(
        "qhd,khd->hqk", queries, keys_all, preferred_element_type=jnp.float32
    ) * head_size ** (-0.5)
    same_image = segment_ids[:, None] == segment_ids[None, :]
    scores = jnp.where(same_image[None, :, :], scores, -1e30)
    top_score = jnp.max(scores, axis=2, keepdims=True)
    expo = jnp.exp(scores - top_score)
    attn_weights = (expo / jnp.sum(expo, axis=2, keepdims=True)).astype(jnp.bfloat16)
    context = jnp.einsum(
        "hqk,khd->qhd", attn_weights, values_all, preferred_element_type=jnp.float32
    )
    return context.reshape(row_count, model_width).astype(jnp.bfloat16)


def merge_and_place(hidden, segment_ids, owners, ln_gain, ln_bias, owner_count, capacity):
    row_count, model_width = hidden.shape
    row_mean = jnp.mean(hidden, axis=1, keepdims=True)
    centered = hidden - row_mean
    row_var = jnp.mean(centered * centered, axis=1, keepdims=True)
    normed = (centered * lax.rsqrt(row_var + 1e-06) * ln_gain[None, :] + ln_bias[None, :]).astype(
        jnp.bfloat16
    )
    merged = normed.reshape(row_count // 4, 4 * model_width)
    live_group = segment_ids.reshape(row_count // 4, 4)[:, 0] < IMGS
    group_ids = jnp.arange(row_count // 4, dtype=jnp.int32)
    earlier = (
        (owners[None, :] == owners[:, None])
        & (group_ids[None, :] < group_ids[:, None])
        & live_group[None, :]
    )
    slot_index = jnp.sum(earlier.astype(jnp.int32), axis=1)
    target = owners * capacity + slot_index
    slot_ids = jnp.arange(owner_count * capacity, dtype=jnp.int32)
    onehot_map = ((slot_ids[:, None] == target[None, :]) & live_group[None, :]).astype(jnp.bfloat16)
    return jnp.dot(onehot_map, merged, preferred_element_type=jnp.float32).astype(jnp.bfloat16)


def body(patches, query_key_value, counts, owner_index, out_weight, ln_gain, ln_bias):
    row_count, model_width = patches.shape
    owner_count = lax.axis_size("seq")
    group_count = row_count // 4
    capacity = max(2, (group_count + owner_count - 1) // owner_count)
    segment_ids = segment_rows(counts[0], row_count)
    context = attend(query_key_value, segment_ids, model_width)
    slice_rows = model_width // owner_count
    own_slice = lax.dynamic_slice_in_dim(
        out_weight, lax.axis_index("seq") * slice_rows, slice_rows, 0
    )
    weight_slab = lax.all_gather(own_slice, "dp", axis=1, tiled=True)
    projected = jnp.dot(
        context,
        lax.all_gather(weight_slab, "seq", axis=0, tiled=True),
        preferred_element_type=jnp.float32,
    )
    hidden = patches.astype(jnp.float32) + projected
    outgoing = merge_and_place(
        hidden, segment_ids, owner_index[:, 0], ln_gain, ln_bias, owner_count, capacity
    )
    outgoing = outgoing.reshape(owner_count, capacity, 4 * model_width)
    received = lax.all_to_all(outgoing, "seq", split_axis=0, concat_axis=0, tiled=True)
    return received.reshape(owner_count * capacity, 4 * model_width)


def solution(mesh):
    placed = (
        P(("dp", "seq"), None),
        P(("dp", "seq"), None),
        P(("dp", "seq"), None),
        P(("dp", "seq"), None),
        P(None, "dp"),
        P(),
        P(),
    )
    return jax.shard_map(
        body, mesh=mesh, in_specs=placed, out_specs=P(("dp", "seq"), None), check_vma=False
    )
```

profile of v0, /device:TPU:0, one launch (start us, length us, event | category | flops | bytes accessed | tf_op | source)
XLA Modules:
  0.0 86.8 jit_solution(10084298187133097372)
XLA Ops:
  6.5 0.0 copy-start
  6.5 0.0 all-gather.3.cloned.1.call-start
  6.5 1.1 %copy-done = bf16[1280,320]{0,1:T(8,128)(2,1)S(1)} copy-done((bf16[1280,320]{0,1:T(8,128)(2,1)S(1)}, bf16[1280,320]{0,1:T(8,128)(2,1)}, u32[]{:S(2)}) %copy-start) | copy-done | bytes 819224
  7.7 0.1 constant_dynamic-slice_fusion
  7.8 0.1 copy.38
  7.9 17.1 %all-gather = bf16[4,320,160]{1,2,0:T(8,128)(2,1)S(1)} all-gather(bf16[1,320,160]{1,2,0:T(8,128)(2,1)S(1)} %bitcast.29), channel_id=1, replica_groups=mesh['dp'=4,'seq'=8] {'dp'}, dimensions={0}, use_global_device_ids=true | all-gather | bytes 512000 | tf_op jit(solution)/shard_map/all_gather | solution.py:70
  25.0 0.3 copy.36
  25.3 0.0 copy-start.6
  25.3 1.1 %reshape.116 = bf16[1280,160]{0,1:T(8,128)(2,1)} reshape(bf16[4,320,160]{1,0,2:T(4,128)(2,1)S(1)} %copy.36) | data formatting | bytes 819200
  26.5 0.0 all-gather.3.cloned.1.call-update
  26.5 0.0 copy-start.5
  26.5 1.4 %fusion.18 = (bf16[192,1280]{1,0:T(8,128)(2,1)S(1)}, bf16[192,1280]{1,0:T(8,128)(2,1)S(1)}, bf16[192,1280]{1,0:T(8,128)(2,1)S(1)}) fusion(bf16[192,3840]{1,0:T(8,128)(2,1)} %param.8), kind=kLoop, calls=%fused_computation.34 | loop fusion | bytes 2949120 | tf_op jit(solution)/shard_map/slice | solution.py:20
  27.9 0.2 copy.31
  28.2 0.2 copy.32
  28.4 0.0 copy-done.6
  28.4 0.2 reduce-window.8
  28.6 1.1 %copy.33 = bf16[192,1280]{0,1:T(8,128)(2,1)} copy(bf16[192,1280]{1,0:T(8,128)(2,1)S(1)} %get-tuple-element.7) | data formatting | bytes 983040 | tf_op jit(solution)/shard_map/slice | solution.py:21
  29.7 0.1 convert_reduce_fusion.1
  29.8 0.1 reshape.108
  29.9 0.1 fusion.13
  30.0 0.0 copy-done.5
  30.0 0.2 convert_reduce_fusion
  30.2 0.1 broadcast_compare_fusion
  30.3 0.0 copy-start.1
  30.3 3.0 %fusion.19 = (f32[16,192]{1,0:T(8,128)S(1)}, f32[16,192,192]{1,2,0:T(8,128)}) fusion(pred[192,192]{0,1:T(8,128)(4,1)S(1)} %broadcast_compare_fusion, bf16[192,16,80]{0,2,1:T(8,128)(2,1)S(1)} %bitcast.26, bf16[192,16,80]{0,2,1:T(8,128)(2,1)S(1)} %bitcast.27), kind=kOutput, calls=%fused_computation.35 | convolution fusion | flops 96731328 | bytes 3391488 | tf_op jit(solution)/shard_map/sub | solution.py:28
  33.3 0.0 copy-done.1
  33.3 0.0 copy-start.2
  33.3 2.4 %fusion.6 = bf16[16,192,80]{1,2,0:T(8,128)(2,1)S(1)} fusion(bf16[192,16,80]{0,2,1:T(8,128)(2,1)S(1)} %bitcast.28, f32[16,192,192]{1,2,0:T(8,128)} %get-tuple-element.9, f32[16,192]{1,0:T(8,128)S(1)} %get-tuple-element.8), kind=kOutput, calls=%fused_computation.11 | convolution fusion | flops 95797248 | bytes 3354624 | tf_op jit(solution)/shard_map/hqk,khd->qhd/dot_general | solution.py:30
  35.7 25.4 %all-gather.3.cloned.1.call-done = bf16[1280,1280]{1,0:T(8,128)(2,1)} async-done(((bf16[160,1280]{1,0:T(8,128)(2,1)}), bf16[1280,1280]{1,0:T(8,128)(2,1)}) %all-gather.3.cloned.1.call-update) | async-done | bytes 3276816 | tf_op jit(solution)/shard_map/all_gather | solution.py:73
  61.1 0.0 copy-done.2
  61.1 0.0 copy-start.3
  61.1 0.0 copy-start.4
  61.1 2.9 %fusion.20 = (f32[192]{0:T(256)S(1)}, f32[192,1280]{1,0:T(8,128)S(1)}) fusion(bf16[192,1280]{0,1:T(8,128)(2,1)S(1)} %bitcast.25, bf16[1280,1280]{1,0:T(8,128)(2,1)} %all-gather.3.cloned.1.call-done, bf16[192,1280]{1,0:T(8,128)(2,1)S(1)} %copy-done.2), kind=kOutput, calls=%fused_computation.36 | convolution fusion | flops 629882688 | bytes 5243648 | tf_op jit(solution)/shard_map/dot_general | solution.py:71
  64.0 0.2 multiply_reduce_fusion
  64.3 0.0 copy-done.3
  64.3 0.0 copy-done.4
  64.3 0.2 add_convert_fusion
  64.6 0.3 reshape.112
  64.9 0.3 convolution_convert_fusion
  65.2 0.2 reshape.113
  65.3 13.7 %all_to_all.5 = bf16[8,6,5120]{2,1,0:T(8,128)(2,1)S(1)} all-to-all(bf16[8,6,5120]{2,1,0:T(8,128)(2,1)S(1)} %reshape.113), channel_id=1, replica_groups=mesh['dp'=4,'seq'=8] {'seq'}, dimensions={0} | all-to-all | bytes 983040 | tf_op jit(solution)/shard_map/all_to_all | solution.py:81
  79.0 1.0 %reshape.114 = bf16[48,5120]{1,0:T(8,128)(2,1)} reshape(bf16[8,6,5120]{2,1,0:T(8,128)(2,1)S(1)} %all_to_all.5) | data formatting | bytes 983040 | tf_op jit(solution)/shard_map/reshape | solution.py:82
  (3 shorter events, 0.0 us)
Async XLA Ops:
  6.5 1.1 %copy-start = (bf16[1280,320]{0,1:T(8,128)(2,1)S(1)}, bf16[1280,320]{0,1:T(8,128)(2,1)}, u32[]{:S(2)}) copy-start(bf16[1280,320]{0,1:T(8,128)(2,1)} %param.11) | copy-start | bytes 2457604
  6.5 54.6 %all-gather.3.cloned.1.call-start = ((), (), s32[]{:S(2)}) async-start(), calls=%async_computation.1 | async-start | bytes 3686400 | tf_op jit(solution)/shard_map/all_gather | solution.py:73
  25.3 3.1 %copy-start.6 = (s32[1,4]{1,0:T(1,128)S(1)}, s32[1,4]{1,0:T(1,128)}, u32[]{:S(2)}) copy-start(s32[1,4]{1,0:T(1,128)} %param.9) | copy-start | bytes 52
  26.5 3.5 %copy-start.5 = (s32[48,1]{0,1:T(1,128)S(1)}, s32[48,1]{0,1:T(1,128)}, u32[]{:S(2)}) copy-start(s32[48,1]{0,1:T(1,128)} %param.10) | copy-start | bytes 580
  30.3 3.0 %copy-start.1 = (bf16[192,1280]{0,1:T(8,128)(2,1)S(1)}, bf16[192,1280]{0,1:T(8,128)(2,1)}, u32[]{:S(2)}) copy-start(bf16[192,1280]{0,1:T(8,128)(2,1)} %copy.33) | copy-start | bytes 1474564
  33.3 27.8 %copy-start.2 = (bf16[192,1280]{1,0:T(8,128)(2,1)S(1)}, bf16[192,1280]{1,0:T(8,128)(2,1)}, u32[]{:S(2)}) copy-start(bf16[192,1280]{1,0:T(8,128)(2,1)} %param.7) | copy-start | bytes 1474564
  61.1 3.2 %copy-start.3 = (f32[1280]{0:T(1024)S(1)}, f32[1280]{0:T(1024)}, u32[]{:S(2)}) copy-start(f32[1280]{0:T(1024)} %param.13) | copy-start | bytes 15364
  61.1 3.2 %copy-start.4 = (f32[1280]{0:T(1024)S(1)}, f32[1280]{0:T(1024)}, u32[]{:S(2)}) copy-start(f32[1280]{0:T(1024)} %param.12) | copy-start | bytes 15364
Sparse Core Ops, SparseCore 0:
  26.6 34.4 all-gather.2
where the time goes:
time: 87 us; the launch traced here: 86.8 us
  blocking collectives  30.8 us (35%)
  waiting for transfers between devices  25.4 us (29%)
  between operations  13.5 us (16%)
  matrix products  8.57 us (10%)
  local copies, waits for them, and re-layouts  7.35 us (8%)
  other arithmetic  1.17 us (1%)
    all_gather x1, waiting for transfers between devices, body(): lax.all_gather(weight_slab, 'seq', axis=0, tiled=True)  25.4 us
    all_gather x1, blocking collectives, body(): weight_slab = lax.all_gather(own_slice, 'dp', axis=1, tiled=True)  17.1 us
    all_to_all x1, blocking collectives, body(): lax.all_to_all(outgoing, 'seq', split_axis=0, concat_axis=0, tiled=True)  13.7 us
    sub x1, matrix products, attend(): expo = jnp.exp(scores - top_score)  2.97 us
    dot_general x1, matrix products, body(): jnp.dot(context, lax.all_gather(weight_slab, 'seq', axis=0, tiled=True),...  2.89 us
    unnamed x16, local copies, waits for them, and re-layouts  2.45 us
    dot_general x1, matrix products, attend(): jnp.einsum('hqk,khd->qhd', attn_weights, values_all, preferred_element_ty...  2.44 us
  transfers between devices with their start and end apart: 1, of which 1 were waited for; matrix products, arithmetic and copies ran while one was open for 11% of the time, Pallas kernels for 0%

commit v1 on v0

--- a/solution.py
+++ b/solution.py
@@ -67,7 +67,16 @@
     own_slice = lax.dynamic_slice_in_dim(
         out_weight, lax.axis_index("seq") * slice_rows, slice_rows, 0
     )
-    weight_slab = lax.all_gather(own_slice, "dp", axis=1, tiled=True)
+    ways = lax.axis_size("dp")
+    up = [(d, (d + 1) % ways) for d in range(ways)]
+    down = [(d, (d - 1) % ways) for d in range(ways)]
+    earlier_2, later = ([own_slice], [own_slice])
+    for _ in range(ways // 2):
+        earlier_2.append(lax.ppermute(earlier_2[-1], "dp", up))
+    for _ in range((ways - 1) // 2):
+        later.append(lax.ppermute(later[-1], "dp", down))
+    line = jnp.concatenate([*earlier_2[::-1], *later[1:]], axis=1)
+    weight_slab = jnp.roll(line, (lax.axis_index("dp") - ways // 2) * own_slice.shape[1], axis=1)
     projected = jnp.dot(
         context,
         lax.all_gather(weight_slab, "seq", axis=0, tiled=True),

time: 87 us -> 83.5 us (0.960)
  blocking collectives: 30.8 us -> 13.7 us
  waiting for transfers between devices: 25.4 us -> 34.6 us
  starting transfers between devices: 0.01 us -> 5.2 us
    all_gather x1 -> x0, blocking collectives: 17.1 us -> none  [body(): weight_slab = lax.all_gather(own_slice, 'dp', axis=1, tiled=True)]
    ppermute x0 -> x3, waiting for transfers between devices: none -> 10.8 us  [the longest x2 9.57 us: body(): earlier_2.append(lax.ppermute(earlier_2[-1], 'dp', up))]
    ppermute x0 -> x3, starting transfers between devices: none -> 5.2 us  [the longest x2 3.11 us: body(): earlier_2.append(lax.ppermute(earlier_2[-1], 'dp', up))]
    all_gather x1, waiting for transfers between devices: 25.4 us -> 23.8 us  [body(): lax.all_gather(weight_slab, 'seq', axis=0, tiled=True)]
    unnamed x16 -> x13, local copies, waits for them, and re-layouts: 2.45 us -> 1.29 us
    dynamic_slice x0 -> x1, local copies, waits for them, and re-layouts: none -> 0.94 us  [body(): jnp.roll(line, (lax.axis_index('dp') - ways // 2) * own_slice.shape[1], a...]
  transfers between devices with their start and end apart: 1 -> 4, of which waited for: 1 -> 4; matrix products, arithmetic and copies ran while one was open for 11% -> 10% of each run, Pallas kernels for 0% -> 0%
where the time goes in v1:
time: 83.5 us; the launch traced here: 83.2 us
  waiting for transfers between devices  34.6 us (41%)
  blocking collectives  13.7 us (16%)
  between operations  13.5 us (16%)
  matrix products  8.57 us (10%)
  local copies, waits for them, and re-layouts  6.52 us (8%)
  starting transfers between devices  5.2 us (6%)
  other arithmetic  1.17 us (1%)
    all_gather x1, waiting for transfers between devices, body(): lax.all_gather(weight_slab, 'seq', axis=0, tiled=True)  23.8 us
    all_to_all x1, blocking collectives, body(): lax.all_to_all(outgoing, 'seq', split_axis=0, concat_axis=0, tiled=True)  13.7 us
    ppermute x2, waiting for transfers between devices, body(): earlier_2.append(lax.ppermute(earlier_2[-1], 'dp', up))  9.57 us
    ppermute x2, starting transfers between devices, body(): earlier_2.append(lax.ppermute(earlier_2[-1], 'dp', up))  3.11 us
    sub x1, matrix products, attend(): expo = jnp.exp(scores - top_score)  2.95 us
    dot_general x1, matrix products, body(): jnp.dot(context, lax.all_gather(weight_slab, 'seq', axis=0, tiled=True),...  2.88 us
    dot_general x1, matrix products, attend(): jnp.einsum('hqk,khd->qhd', attn_weights, values_all, preferred_element_ty...  2.48 us
    ppermute x1, starting transfers between devices, body(): later.append(lax.ppermute(later[-1], 'dp', down))  2.09 us
  transfers between devices with their start and end apart: 4, of which 4 were waited for; matrix products, arithmetic and copies ran while one was open for 10% of the time, Pallas kernels for 0%

profile of v1, /device:TPU:0, one launch (start us, length us, event | category | flops | bytes accessed | tf_op | source)
XLA Modules:
  0.0 83.2 jit_solution(1255777648605047926)
XLA Ops:
  6.5 0.0 copy-start
  6.5 0.0 all-gather.2.cloned.1.call-start
  6.5 1.1 %copy-done = bf16[1280,320]{0,1:T(8,128)(2,1)S(1)} copy-done((bf16[1280,320]{0,1:T(8,128)(2,1)S(1)}, bf16[1280,320]{0,1:T(8,128)(2,1)}, u32[]{:S(2)}) %copy-start) | copy-done | bytes 819224
  7.7 0.1 constant_dynamic-slice_fusion.1
  7.8 0.1 copy.31
  7.9 3.1 %collective-permute-start = (bf16[160,320]{1,0:T(8,128)(2,1)S(1)}, bf16[160,320]{1,0:T(8,128)(2,1)S(1)}, u32[]{:S(2)}, u32[]{:S(2)}) collective-permute-start(bf16[160,320]{1,0:T(8,128)(2,1)S(1)} %copy.31), channel_id=1, source_target_pairs={{0,8},{8,16},{16,24},{24,0},{1,9},{9,17},{17,25},{25,1},{2,10},{10... | collective-permute-start | bytes 307208 | tf_op jit(solution)/shard_map/ppermute | solution.py:75
  11.0 2.1 %collective-permute-start.2 = (bf16[160,320]{1,0:T(8,128)(2,1)S(1)}, bf16[160,320]{1,0:T(8,128)(2,1)S(1)}, u32[]{:S(2)}, u32[]{:S(2)}) collective-permute-start(bf16[160,320]{1,0:T(8,128)(2,1)S(1)} %copy.31), channel_id=1, source_target_pairs={{0,24},{8,0},{16,8},{24,16},{1,25},{9,1},{17,9},{25,17},{2,26},{10... | collective-permute-start | bytes 307208 | tf_op jit(solution)/shard_map/ppermute | solution.py:77
  13.1 4.1 %collective-permute-done = bf16[160,320]{1,0:T(8,128)(2,1)S(1)} collective-permute-done((bf16[160,320]{1,0:T(8,128)(2,1)S(1)}, bf16[160,320]{1,0:T(8,128)(2,1)S(1)}, u32[]{:S(2)}, u32[]{:S(2)}) %collective-permute-start) | collective-permute-done | bytes 102432 | tf_op jit(solution)/shard_map/ppermute | solution.py:75
  17.2 0.0 collective-permute-start.1
  17.2 0.0 copy-start.5
  17.2 1.2 %collective-permute-done.2 = bf16[160,320]{1,0:T(8,128)(2,1)S(1)} collective-permute-done((bf16[160,320]{1,0:T(8,128)(2,1)S(1)}, bf16[160,320]{1,0:T(8,128)(2,1)S(1)}, u32[]{:S(2)}, u32[]{:S(2)}) %collective-permute-start.2) | collective-permute-done | bytes 102432 | tf_op jit(solution)/shard_map/ppermute | solution.py:77
  18.5 5.5 %collective-permute-done.1 = bf16[160,320]{1,0:T(8,128)(2,1)S(1)} collective-permute-done((bf16[160,320]{1,0:T(8,128)(2,1)S(1)}, bf16[160,320]{1,0:T(8,128)(2,1)S(1)}, u32[]{:S(2)}, u32[]{:S(2)}) %collective-permute-start.1) | collective-permute-done | bytes 102432 | tf_op jit(solution)/shard_map/ppermute | solution.py:75
  23.9 0.5 concatenate.6
  24.4 0.9 %constant_dynamic-slice_fusion = bf16[160,1280]{1,0:T(8,128)(2,1)} fusion(bf16[160,2560]{1,0:T(8,128)(2,1)S(1)} %concatenate.6, s32[]{:T(128)S(6)} %select_n.23), kind=kLoop, calls=%fused_computation.30 | loop fusion | bytes 819204 | tf_op jit(solution)/shard_map/jit(_roll_dynamic)/dynamic_slice | solution.py:79
  25.4 0.0 all-gather.2.cloned.1.call-update
  25.4 0.0 copy-start.4
  25.4 1.4 %fusion.18 = (bf16[192,1280]{1,0:T(8,128)(2,1)S(1)}, bf16[192,1280]{1,0:T(8,128)(2,1)S(1)}, bf16[192,1280]{1,0:T(8,128)(2,1)S(1)}) fusion(bf16[192,3840]{1,0:T(8,128)(2,1)} %param.8), kind=kLoop, calls=%fused_computation.35 | loop fusion | bytes 2949120 | tf_op jit(solution)/shard_map/slice | solution.py:20
  26.8 0.2 copy.27
  27.1 0.0 copy-done.5
  27.1 0.2 reduce-window.8
  27.3 0.2 copy.25
  27.5 0.2 copy.26
  27.7 0.1 convert_reduce_fusion.1
  27.8 0.1 reshape.108
  27.9 0.1 fusion.13
  28.1 0.0 copy-done.4
  28.1 0.2 convert_reduce_fusion
  28.3 0.1 broadcast_compare_fusion
  28.4 2.9 %fusion.19 = (f32[16,192]{1,0:T(8,128)S(1)}, f32[16,192,192]{1,2,0:T(8,128)}) fusion(pred[192,192]{0,1:T(8,128)(4,1)S(1)} %broadcast_compare_fusion, bf16[192,16,80]{0,2,1:T(8,128)(2,1)S(1)} %bitcast.20, bf16[192,16,80]{0,2,1:T(8,128)(2,1)S(1)} %bitcast.21), kind=kOutput, calls=%fused_computation.36 | convolution fusion | flops 96731328 | bytes 3391488 | tf_op jit(solution)/shard_map/sub | solution.py:28
  31.3 0.0 copy-start.1
  31.3 2.5 %fusion.6 = bf16[16,192,80]{1,2,0:T(8,128)(2,1)S(1)} fusion(bf16[192,16,80]{0,2,1:T(8,128)(2,1)S(1)} %bitcast.19, f32[16,192,192]{1,2,0:T(8,128)} %get-tuple-element.9, f32[16,192]{1,0:T(8,128)S(1)} %get-tuple-element.8), kind=kOutput, calls=%fused_computation.11 | convolution fusion | flops 95797248 | bytes 3354624 | tf_op jit(solution)/shard_map/hqk,khd->qhd/dot_general | solution.py:30
  33.8 23.8 %all-gather.2.cloned.1.call-done = bf16[1280,1280]{1,0:T(8,128)(2,1)} async-done(((bf16[160,1280]{1,0:T(8,128)(2,1)}), bf16[1280,1280]{1,0:T(8,128)(2,1)}) %all-gather.2.cloned.1.call-update) | async-done | bytes 3276816 | tf_op jit(solution)/shard_map/all_gather | solution.py:82
  57.6 0.0 copy-done.1
  57.6 0.0 copy-start.2
  57.6 0.0 copy-start.3
  57.6 2.9 %fusion.20 = (f32[192]{0:T(256)S(1)}, f32[192,1280]{1,0:T(8,128)S(1)}) fusion(bf16[192,1280]{0,1:T(8,128)(2,1)S(1)} %bitcast.18, bf16[1280,1280]{1,0:T(8,128)(2,1)} %all-gather.2.cloned.1.call-done, bf16[192,1280]{1,0:T(8,128)(2,1)S(1)} %copy-done.1), kind=kOutput, calls=%fused_computation.37 | convolution fusion | flops 629882688 | bytes 5243648 | tf_op jit(solution)/shard_map/dot_general | solution.py:80
  60.5 0.2 multiply_reduce_fusion
  60.7 0.0 copy-done.2
  60.7 0.0 copy-done.3
  60.8 0.2 add_convert_fusion
  61.0 0.3 reshape.112
  61.3 0.3 convolution_convert_fusion
  61.6 0.2 reshape.113
  61.8 13.7 %all_to_all.5 = bf16[8,6,5120]{2,1,0:T(8,128)(2,1)S(1)} all-to-all(bf16[8,6,5120]{2,1,0:T(8,128)(2,1)S(1)} %reshape.113), channel_id=1, replica_groups=mesh['dp'=4,'seq'=8] {'seq'}, dimensions={0} | all-to-all | bytes 983040 | tf_op jit(solution)/shard_map/all_to_all | solution.py:90
  75.4 1.0 %reshape.114 = bf16[48,5120]{1,0:T(8,128)(2,1)} reshape(bf16[8,6,5120]{2,1,0:T(8,128)(2,1)S(1)} %all_to_all.5) | data formatting | bytes 983040 | tf_op jit(solution)/shard_map/reshape | solution.py:91
  (3 shorter events, 0.0 us)
Async XLA Ops:
  6.5 1.1 %copy-start = (bf16[1280,320]{0,1:T(8,128)(2,1)S(1)}, bf16[1280,320]{0,1:T(8,128)(2,1)}, u32[]{:S(2)}) copy-start(bf16[1280,320]{0,1:T(8,128)(2,1)} %param.11) | copy-start | bytes 2457604
  6.5 51.0 %all-gather.2.cloned.1.call-start = ((), (), s32[]{:S(2)}) async-start(), calls=%async_computation.1 | async-start | bytes 3686400 | tf_op jit(solution)/shard_map/all_gather | solution.py:82
  7.9 9.3 %collective-permute-start = (bf16[160,320]{1,0:T(8,128)(2,1)S(1)}, bf16[160,320]{1,0:T(8,128)(2,1)S(1)}, u32[]{:S(2)}, u32[]{:S(2)}) collective-permute-start(bf16[160,320]{1,0:T(8,128)(2,1)S(1)} %copy.31), channel_id=1, source_target_pairs={{0,8},{8,16},{16,24},{24,0},{1,9},{9,17},{17,25},{25,1},{2,10},{10... | collective-permute-start | bytes 307208 | tf_op jit(solution)/shard_map/ppermute | solution.py:75
  11.0 7.4 %collective-permute-start.2 = (bf16[160,320]{1,0:T(8,128)(2,1)S(1)}, bf16[160,320]{1,0:T(8,128)(2,1)S(1)}, u32[]{:S(2)}, u32[]{:S(2)}) collective-permute-start(bf16[160,320]{1,0:T(8,128)(2,1)S(1)} %copy.31), channel_id=1, source_target_pairs={{0,24},{8,0},{16,8},{24,16},{1,25},{9,1},{17,9},{25,17},{2,26},{10... | collective-permute-start | bytes 307208 | tf_op jit(solution)/shard_map/ppermute | solution.py:77
  17.2 6.7 %collective-permute-start.1 = (bf16[160,320]{1,0:T(8,128)(2,1)S(1)}, bf16[160,320]{1,0:T(8,128)(2,1)S(1)}, u32[]{:S(2)}, u32[]{:S(2)}) collective-permute-start(bf16[160,320]{1,0:T(8,128)(2,1)S(1)} %collective-permute-done), channel_id=1, source_target_pairs={{0,8},{8,16},{16,24},{24,0},{1,9},{9,17},{17,25},{25,1},{2,10},{10... | collective-permute-start | bytes 307208 | tf_op jit(solution)/shard_map/ppermute | solution.py:75
  17.2 9.8 %copy-start.5 = (s32[1,4]{1,0:T(1,128)S(1)}, s32[1,4]{1,0:T(1,128)}, u32[]{:S(2)}) copy-start(s32[1,4]{1,0:T(1,128)} %param.9) | copy-start | bytes 52
  25.4 2.7 %copy-start.4 = (s32[48,1]{0,1:T(1,128)S(1)}, s32[48,1]{0,1:T(1,128)}, u32[]{:S(2)}) copy-start(s32[48,1]{0,1:T(1,128)} %param.10) | copy-start | bytes 580
  31.3 26.3 %copy-start.1 = (bf16[192,1280]{1,0:T(8,128)(2,1)S(1)}, bf16[192,1280]{1,0:T(8,128)(2,1)}, u32[]{:S(2)}) copy-start(bf16[192,1280]{1,0:T(8,128)(2,1)} %param.7) | copy-start | bytes 1474564
  57.6 3.2 %copy-start.2 = (f32[1280]{0:T(1024)S(1)}, f32[1280]{0:T(1024)}, u32[]{:S(2)}) copy-start(f32[1280]{0:T(1024)} %param.13) | copy-start | bytes 15364
  57.6 3.2 %copy-start.3 = (f32[1280]{0:T(1024)S(1)}, f32[1280]{0:T(1024)}, u32[]{:S(2)}) copy-start(f32[1280]{0:T(1024)} %param.12) | copy-start | bytes 15364
Sparse Core Ops, SparseCore 0:
  25.5 32.0 all-gather.1
